TPU v7x, 32 devices: a whole 2x2x4 slice. The times are simulated.
32 devices in a mesh: grp: 2 (over core), dp: 4 (over y, x), sp: 4 (over z).
Axes of the slice: x: 2, y: 2, z: 4, core: 2. Of those that a mesh axis runs over, the one named last changes fastest.
Arguments:
- vis: bfloat16 [512, 5120], P(('grp', 'dp', 'sp')), may hold values from -6 to 6
- merge_weight: bfloat16 [5120, 8192], P('dp', ('grp', 'sp')), may hold values from -0.078125 to 0.078125
- img_counts: int32 [32], P('dp'), may hold values from 1 to 16
- img_pos: int32 [512], P(('grp', 'dp', 'sp')), may hold values from 0 to 127, as said below
- text: bfloat16 [4096, 8192], P(('grp', 'dp', 'sp')), may hold values from -6 to 6
- cot: bfloat16 [4096, 8192], P(('grp', 'dp', 'sp')), may hold values from -6 to 6
- gain: float32 [8192], replicated, may hold values from 0.25 to 1.75
Outputs:
- vis_grad: bfloat16 [512, 5120], P(('grp', 'dp', 'sp'))
- gain_grad: float32 [8192], replicated
Inputs may be any that keep to these rules, and one draw needn't show every extreme that they name: `img_pos`: within one device's block the 16 positions are distinct. `img_counts`: the counts of one image group sum to at most 128.
All inputs are finite; a program needn't handle non-finite values.
Results may differ from a plain program's by a relative error of at most 0.014.
Values may be sent and summed in bfloat16 or wider, within the bound.
No kernel may reach another device: no remote copies, remote signals or barrier semaphores. Data moves between devices by JAX's collectives and lax.ppermute only.
A program may use at most 128 MiB of HBM per device.

v0:
```python
import jax
import jax.numpy as jnp
from jax import lax
from jax.sharding import PartitionSpec as P


def body(vis, merge_weight, img_counts, img_pos, text, cot, gain):
    rows_dev = vis.shape[0]
    tok_rows = text.shape[0]
    group_vis = lax.all_gather(vis, ("grp", "sp"), axis=0, tiled=True)
    full_weight = lax.all_gather(merge_weight, "dp", axis=0, tiled=True)
    partial_value = jnp.dot(group_vis, full_weight, preferred_element_type=jnp.float32)
    emb = lax.all_to_all(
        partial_value.astype(jnp.bfloat16), ("grp", "sp"), split_axis=0, concat_axis=1, tiled=True
    )
    total_live = jnp.sum(img_counts)
    member = lax.axis_index("grp") * lax.axis_size("sp") + lax.axis_index("sp")
    group_row = member * rows_dev + jnp.arange(rows_dev, dtype=jnp.int32)
    live = group_row < total_live
    places = jnp.arange(tok_rows, dtype=jnp.int32)
    select = (img_pos[None, :] == places[:, None]) & live[None, :]
    taken = jnp.any(select, axis=1)
    select_b = select.astype(jnp.bfloat16)
    placed = jnp.dot(select_b, emb, preferred_element_type=jnp.float32)
    hidden = jnp.where(taken[:, None], placed, text.astype(jnp.float32))
    rinv = lax.rsqrt(jnp.mean(hidden * hidden, axis=1, keepdims=True) + 1e-06)
    cotf = cot.astype(jnp.float32)
    part_gain = jnp.sum(cotf * hidden * rinv, axis=0)
    scaled = cotf * gain[None, :]
    inner = jnp.mean(scaled * hidden, axis=1, keepdims=True)
    dhid = (rinv * scaled - hidden * rinv**3 * inner).astype(jnp.bfloat16)
    demb = jnp.dot(select_b.T, dhid, preferred_element_type=jnp.float32)
    demb = jnp.where(live[:, None], demb, 0.0).astype(jnp.bfloat16)
    returned = lax.all_to_all(demb, ("grp", "sp"), split_axis=1, concat_axis=0, tiled=True)
    terms = lax.dot_general(
        returned, full_weight, (((1,), (1,)), ((), ())), preferred_element_type=jnp.float32
    )
    vis_grad = lax.psum_scatter(
        terms.astype(jnp.bfloat16), ("grp", "sp"), scatter_dimension=0, tiled=True
    )
    gain_grad = lax.psum(part_gain, ("grp", "dp", "sp"))
    return (vis_grad, gain_grad)


def solution(mesh):
    return jax.shard_map(
        body,
        mesh=mesh,
        in_specs=(
            P(("grp", "dp", "sp"), None),
            P("dp", ("grp", "sp")),
            P("dp"),
            P(("grp", "dp", "sp")),
            P(("grp", "dp", "sp"), None),
            P(("grp", "dp", "sp"), None),
            P(),
        ),
        out_specs=(P(("grp", "dp", "sp"), None), P()),
        check_vma=False,
    )
```

profile of v0, /device:TPU:0, one launch (start us, length us, event | category | flops | bytes accessed | tf_op | source)
XLA Modules:
  0.0 229.6 jit_solution(17347707635758896386)
XLA Ops:
  7.2 0.0 all-gather.3.cloned.1.call-start
  7.2 0.7 all-gather.3.cloned.1.call-update
  7.9 0.0 all-gather.5.cloned.1.call-start
  7.9 0.7 all-gather.5.cloned.1.call-update
  8.6 0.0 copy-start.4
  8.7 0.0 copy-start.3
  8.7 0.0 copy-start
  8.7 27.1 %all-gather.3.cloned.1.call-done = bf16[128,5120]{1,0:T(8,128)(2,1)} async-done(((bf16[16,5120]{1,0:T(8,128)(2,1)}), bf16[128,5120]{1,0:T(8,128)(2,1)}) %all-gather.3.cloned.1.call-update) | async-done | bytes 1310736 | tf_op jit(solution)/shard_map/all_gather | solution.py:10
  35.7 106.3 %all-gather.5.cloned.1.call-done = bf16[5120,1024]{1,0:T(8,128)(2,1)} async-done(((bf16[1280,1024]{1,0:T(8,128)(2,1)}), bf16[5120,1024]{1,0:T(8,128)(2,1)}) %all-gather.5.cloned.1.call-update) | async-done | bytes 10485776 | tf_op jit(solution)/shard_map/all_gather | solution.py:11
  142.1 6.6 %convolution_convert_fusion.1 = bf16[128,1024]{1,0:T(8,128)(2,1)} fusion(bf16[128,5120]{1,0:T(8,128)(2,1)} %all-gather.3.cloned.1.call-done, bf16[5120,1024]{1,0:T(8,128)(2,1)} %all-gather.5.cloned.1.call-done), kind=kOutput, calls=%fused_computation.14 | convolution fusion | flops 1342308352 | bytes 12058624 | tf_op jit(solution)/shard_map/dot_general | solution.py:12
  148.7 0.0 copy-start.2
  148.7 4.7 %all-to-all-start = ((bf16[8,16,1024]{2,1,0:T(8,128)(2,1)}), bf16[8,16,1024]{2,1,0:T(8,128)(2,1)S(1)}, u32[]{:S(2)}, u32[]{:S(2)}) async-start(bf16[8,16,1024]{2,1,0:T(8,128)(2,1)} %bitcast), calls=%async_computation | async-start | bytes 524288 | tf_op jit(solution)/shard_map/all_to_all | solution.py:13
  153.4 0.0 reduce-scatter.2.cloned.1.call-start
  153.5 0.0 copy-done.4
  153.5 0.6 reduce_sum.36
  154.1 0.7 add_compare_fusion
  154.8 0.0 copy-done.3
  154.8 0.1 fusion.12
  154.9 7.9 %all-to-all-done = bf16[8,16,1024]{2,1,0:T(8,128)(2,1)S(1)} async-done(((bf16[8,16,1024]{2,1,0:T(8,128)(2,1)}), bf16[8,16,1024]{2,1,0:T(8,128)(2,1)S(1)}, u32[]{:S(2)}, u32[]{:S(2)}) %all-to-all-start) | async-done | bytes 262176 | tf_op jit(solution)/shard_map/all_to_all | solution.py:13
  162.8 0.0 copy-start.1
  162.8 0.0 copy-done
  162.8 0.0 slice-start
  162.8 1.0 multiply_reduce_fusion
  163.8 0.0 copy-done.2
  163.8 0.6 copy-done.1
  164.4 0.0 slice-start.1
  164.4 1.5 fusion.7
  165.9 0.0 slice-start.2
  165.9 1.1 fusion
  167.1 11.8 %all_to_all.38 = bf16[16,8,1024]{2,0,1:T(8,128)(2,1)S(1)} all-to-all(bf16[16,8,1024]{2,0,1:T(8,128)(2,1)S(1)} %bitcast.21), channel_id=1, replica_groups=mesh['grp'=2,'dp'=4,'sp'=4] {'grp','sp'}, dimensions={1} | all-to-all | bytes 524288 | tf_op jit(solution)/shard_map/all_to_all | solution.py:34
  178.8 0.0 slice-done
  178.9 0.0 slice-done.1
  178.9 0.0 slice-done.2
  178.9 4.6 %convolution_convert_fusion = bf16[128,5120]{1,0:T(8,128)(2,1)} fusion(bf16[128,1024]{1,0:T(8,128)(2,1)S(1)} %bitcast.19, bf16[5120,1024]{1,0:T(8,128)(2,1)S(1)} %bitcast.17), kind=kOutput, calls=%fused_computation.3 | convolution fusion | flops 1342832640 | bytes 12058624 | tf_op jit(solution)/shard_map/dot_general | solution.py:35
  183.5 0.0 reduce-scatter.2.cloned.1.call-update
  183.5 39.5 %psum.7 = f32[8192]{0:T(1024)} all-reduce(f32[8192]{0:T(1024)S(1)} %get-tuple-element.2), channel_id=1, replica_groups=mesh['grp'=2,'dp'=4,'sp'=4] {'grp','dp','sp'}, use_global_device_ids=true, to_apply=%region_6.7 | all-reduce | flops 8192 | bytes 65536 | tf_op jit(solution)/shard_map/psum | solution.py:41
  223.0 0.0 reduce-scatter.2.cloned.1.call-done
  (5 shorter events, 0.1 us)
Async XLA Ops:
  7.2 28.6 %all-gather.3.cloned.1.call-start = ((), (), s32[]{:S(2)}) async-start(), calls=%async_computation.3 | async-start | bytes 1474560 | tf_op jit(solution)/shard_map/all_gather | solution.py:10
  7.9 134.2 %all-gather.5.cloned.1.call-start = ((), (), s32[]{:S(2)}) async-start(), calls=%async_computation.4 | async-start | bytes 13107200 | tf_op jit(solution)/shard_map/all_gather | solution.py:11
  8.6 144.8 %copy-start.4 = (s32[8]{0:T(128)S(1)}, s32[8]{0:T(128)}, u32[]{:S(2)}) copy-start(s32[8]{0:T(128)} %param.9) | copy-start | bytes 100
  8.7 146.1 %copy-start.3 = (s32[16]{0:T(128)S(1)}, s32[16]{0:T(128)}, u32[]{:S(2)}) copy-start(s32[16]{0:T(128)} %param.10) | copy-start | bytes 196
  8.7 154.1 %copy-start = (bf16[128,8192]{1,0:T(8,128)(2,1)S(1)}, bf16[128,8192]{1,0:T(8,128)(2,1)}, u32[]{:S(2)}) copy-start(bf16[128,8192]{1,0:T(8,128)(2,1)} %param.11) | copy-start | bytes 6291460
  148.7 15.1 %copy-start.2 = (f32[8192]{0:T(1024)S(1)}, f32[8192]{0:T(1024)}, u32[]{:S(2)}) copy-start(f32[8192]{0:T(1024)} %param.13) | copy-start | bytes 98308
  148.7 14.1 %all-to-all-start = ((bf16[8,16,1024]{2,1,0:T(8,128)(2,1)}), bf16[8,16,1024]{2,1,0:T(8,128)(2,1)S(1)}, u32[]{:S(2)}, u32[]{:S(2)}) async-start(bf16[8,16,1024]{2,1,0:T(8,128)(2,1)} %bitcast), calls=%async_computation | async-start | bytes 524288 | tf_op jit(solution)/shard_map/all_to_all | solution.py:13
  153.4 69.6 %reduce-scatter.2.cloned.1.call-start = ((), (), s32[]{:S(2)}) async-start(), calls=%async_computation.5 | async-start | bytes 1474560 | tf_op jit(solution)/shard_map/reduce_scatter | solution.py:38
  162.8 1.6 copy-start.1
  162.8 16.0 %slice-start = ((s8[10485760]{0:T(1024)(128)(4,1)}), s8[4194304]{0:T(1024)(128)(4,1)S(1)}, s32[]{:S(2)}) async-start(s8[10485760]{0:T(1024)(128)(4,1)} %bitcast.16), calls=%async_computation.6 | async-start | bytes 8388608
  164.4 14.5 %slice-start.1 = ((s8[10485760]{0:T(1024)(128)(4,1)}), s8[4194304]{0:T(1024)(128)(4,1)S(1)}, s32[]{:S(2)}) async-start(s8[10485760]{0:T(1024)(128)(4,1)} %bitcast.16), calls=%async_computation.7 | async-start | bytes 8388608
  165.9 13.0 %slice-start.2 = ((s8[10485760]{0:T(1024)(128)(4,1)}), s8[2097152]{0:T(1024)(128)(4,1)S(1)}, s32[]{:S(2)}) async-start(s8[10485760]{0:T(1024)(128)(4,1)} %bitcast.16), calls=%async_computation.8 | async-start | bytes 4194304
Sparse Core Ops, SparseCore 0:
  9.6 26.1 all-gather.2
  37.6 104.4 all-gather.4
  183.6 34.8 reduce-scatter.1
where the time goes:
time: 230 us
  waiting for transfers between devices  143 us (62%)
  blocking collectives  51.3 us (22%)
  between operations  13.9 us (6%)
  matrix products  13.4 us (6%)
  starting transfers between devices  4.85 us (2%)
  other arithmetic  2.91 us (1%)
    all_gather x1, waiting for transfers between devices, body(): full_weight = lax.all_gather(merge_weight, 'dp', axis=0, tiled=True)  106 us
    psum x1, blocking collectives, body(): gain_grad = lax.psum(part_gain, ('grp', 'dp', 'sp'))  39.5 us
    all_gather x1, waiting for transfers between devices, body(): group_vis = lax.all_gather(vis, ('grp', 'sp'), axis=0, tiled=True)  27.1 us
    all_to_all x1, blocking collectives, body(): lax.all_to_all(demb, ('grp', 'sp'), split_axis=1, concat_axis=0, tiled=True)  11.8 us
    all_to_all x1, waiting for transfers between devices, body(): lax.all_to_all(partial_value.astype(jnp.bfloat16), ('grp', 'sp'), split_a...  7.9 us
    dot_general x1, matrix products, body(): jnp.dot(group_vis, full_weight, preferred_element_type=jnp.float32)  6.62 us
    all_to_all x1, starting transfers between devices, body(): lax.all_to_all(partial_value.astype(jnp.bfloat16), ('grp', 'sp'), split_a...  4.74 us
    dot_general x1, matrix products, body(): lax.dot_general(returned, full_weight, (((1,), (1,)), ((), ())), preferre...  4.62 us
  transfers between devices with their start and end apart: 4, of which 3 were waited for; matrix products, arithmetic and copies ran while one was open for 1% of the time, Pallas kernels for 0%

commit v1 on v0

--- a/solution.py
+++ b/solution.py
@@ -7,7 +7,15 @@
 def body(vis, merge_weight, img_counts, img_pos, text, cot, gain):
     rows_dev = vis.shape[0]
     tok_rows = text.shape[0]
-    group_vis = lax.all_gather(vis, ("grp", "sp"), axis=0, tiled=True)
+    ways, here = (lax.axis_size(("grp", "sp")), lax.axis_index(("grp", "sp")))
+    grown, reach = (vis, 1)
+    while reach < ways:
+        theirs = lax.ppermute(grown, ("grp", "sp"), [(d, d ^ reach) for d in range(ways)])
+        mine_first = jnp.concatenate([grown, theirs], axis=0)
+        theirs_first = jnp.concatenate([theirs, grown], axis=0)
+        grown = jnp.where(here & reach == 0, mine_first, theirs_first)
+        reach = 2 * reach
+    group_vis = grown
     full_weight = lax.all_gather(merge_weight, "dp", axis=0, tiled=True)
     partial_value = jnp.dot(group_vis, full_weight, preferred_element_type=jnp.float32)
     emb = lax.all_to_all(

time: 230 us -> 205 us (0.89)
  waiting for transfers between devices: 143 us -> 111 us
  starting transfers between devices: 4.85 us -> 10.8 us
    all_gather x1 -> x0, waiting for transfers between devices: 27.1 us -> none  [body(): group_vis = lax.all_gather(vis, ('grp', 'sp'), axis=0, tiled=True)]
    all_gather x1, waiting for transfers between devices: 106 us -> 81.9 us  [body(): full_weight = lax.all_gather(merge_weight, 'dp', axis=0, tiled=True)]
    ppermute x0 -> x3, waiting for transfers between devices: none -> 20.5 us  [body(): lax.ppermute(grown, ('grp', 'sp'), [(d, d ^ reach) for d in range(ways)])]
    ppermute x0 -> x3, starting transfers between devices: none -> 6.01 us  [body(): lax.ppermute(grown, ('grp', 'sp'), [(d, d ^ reach) for d in range(ways)])]
  transfers between devices with their start and end apart: 4 -> 6, of which waited for: 3 -> 5; matrix products, arithmetic and copies ran while one was open for 1% -> 1% of each run, Pallas kernels for 0% -> 0%
where the time goes in v1:
time: 205 us
  waiting for transfers between devices  111 us (54%)
  blocking collectives  51.3 us (25%)
  between operations  14.2 us (7%)
  matrix products  13 us (6%)
  starting transfers between devices  10.8 us (5%)
  other arithmetic  4.08 us (2%)
    all_gather x1, waiting for transfers between devices, body(): full_weight = lax.all_gather(merge_weight, 'dp', axis=0, tiled=True)  81.9 us
    psum x1, blocking collectives, body(): gain_grad = lax.psum(part_gain, ('grp', 'dp', 'sp'))  39.6 us
    ppermute x3, waiting for transfers between devices, body(): lax.ppermute(grown, ('grp', 'sp'), [(d, d ^ reach) for d in range(ways)])  20.5 us
    all_to_all x1, blocking collectives, body(): lax.all_to_all(demb, ('grp', 'sp'), split_axis=1, concat_axis=0, tiled=True)  11.8 us
    all_to_all x1, waiting for transfers between devices, body(): lax.all_to_all(partial_value.astype(jnp.bfloat16), ('grp', 'sp'), split_a...  7.91 us
    dot_general x1, matrix products, body(): jnp.dot(group_vis, full_weight, preferred_element_type=jnp.float32)  6.23 us
    ppermute x3, starting transfers between devices, body(): lax.ppermute(grown, ('grp', 'sp'), [(d, d ^ reach) for d in range(ways)])  6.01 us
    all_to_all x1, starting transfers between devices, body(): lax.all_to_all(partial_value.astype(jnp.bfloat16), ('grp', 'sp'), split_a...  4.73 us
  transfers between devices with their start and end apart: 6, of which 5 were waited for; matrix products, arithmetic and copies ran while one was open for 1% of the time, Pallas kernels for 0%

profile of v1, /device:TPU:0, one launch (start us, length us, event | category | flops | bytes accessed | tf_op | source)
XLA Modules:
  0.0 205.0 jit_solution(11279214499522345765)
XLA Ops:
  7.2 0.0 all-gather.2.cloned.1.call-start
  7.2 0.7 all-gather.2.cloned.1.call-update
  7.9 3.1 %collective-permute-start = (bf16[16,5120]{1,0:T(8,128)(2,1)}, bf16[16,5120]{1,0:T(8,128)(2,1)S(1)}, u32[]{:S(2)}, u32[]{:S(2)}) collective-permute-start(bf16[16,5120]{1,0:T(8,128)(2,1)} %param.7), channel_id=1, source_target_pairs={{0,1},{1,0},{2,3},{3,2},{16,17},{17,16},{18,19},{19,18},{4,5},{5,4... | collective-permute-start | bytes 491528 | tf_op jit(solution)/shard_map/ppermute | solution.py:13
  11.0 4.4 %collective-permute-done = bf16[16,5120]{1,0:T(8,128)(2,1)S(1)} collective-permute-done((bf16[16,5120]{1,0:T(8,128)(2,1)}, bf16[16,5120]{1,0:T(8,128)(2,1)S(1)}, u32[]{:S(2)}, u32[]{:S(2)}) %collective-permute-start) | collective-permute-done | bytes 163872 | tf_op jit(solution)/shard_map/ppermute | solution.py:13
  15.4 1.1 maximum_select_fusion.5
  16.5 2.8 %collective-permute-start.1 = (bf16[32,5120]{1,0:T(8,128)(2,1)S(1)}, bf16[32,5120]{1,0:T(8,128)(2,1)S(1)}, u32[]{:S(2)}, u32[]{:S(2)}) collective-permute-start(bf16[32,5120]{1,0:T(8,128)(2,1)S(1)} %maximum_select_fusion.5), channel_id=1, source_target_pairs={{0,2},{1,3},{2,0},{3,1},{16,18},{17,19},{18,16},{19,17},{4,6},{5,7... | collective-permute-start | bytes 983048 | tf_op jit(solution)/shard_map/ppermute | solution.py:13
  19.3 14.0 %collective-permute-done.1 = bf16[32,5120]{1,0:T(8,128)(2,1)S(1)} collective-permute-done((bf16[32,5120]{1,0:T(8,128)(2,1)S(1)}, bf16[32,5120]{1,0:T(8,128)(2,1)S(1)}, u32[]{:S(2)}, u32[]{:S(2)}) %collective-permute-start.1) | collective-permute-done | bytes 327712 | tf_op jit(solution)/shard_map/ppermute | solution.py:13
  33.4 0.1 maximum_select_fusion.4
  33.5 0.1 collective-permute-start.2
  33.5 0.0 copy-start.4
  33.6 0.0 copy-start.3
  33.6 0.0 copy-start
  33.6 2.0 collective-permute-done.2
  35.6 81.9 %all-gather.2.cloned.1.call-done = bf16[5120,1024]{1,0:T(8,128)(2,1)} async-done(((bf16[1280,1024]{1,0:T(8,128)(2,1)}), bf16[5120,1024]{1,0:T(8,128)(2,1)}) %all-gather.2.cloned.1.call-update) | async-done | bytes 10485776 | tf_op jit(solution)/shard_map/all_gather | solution.py:19
  117.5 6.2 %fusion.16 = bf16[128,1024]{1,0:T(8,128)(2,1)} fusion(bf16[5120,1024]{1,0:T(8,128)(2,1)} %all-gather.2.cloned.1.call-done, bf16[64,5120]{1,0:T(8,128)(2,1)S(1)} %collective-permute-done.2, bf16[64,5120]{1,0:T(8,128)(2,1)S(1)} %maximum_select_fusion.4, pred[]{:T(512)S(6)} %eq.25), kind=kOutput, calls=%fused_computation.22 | convolution fusion | flops 1348206592 | bytes 12058625 | tf_op jit(solution)/shard_map/dot_general | solution.py:20
  123.7 0.0 copy-start.2
  123.7 4.7 %all-to-all-start = ((bf16[8,16,1024]{2,1,0:T(8,128)(2,1)}), bf16[8,16,1024]{2,1,0:T(8,128)(2,1)S(1)}, u32[]{:S(2)}, u32[]{:S(2)}) async-start(bf16[8,16,1024]{2,1,0:T(8,128)(2,1)} %bitcast), calls=%async_computation | async-start | bytes 524288 | tf_op jit(solution)/shard_map/all_to_all | solution.py:21
  128.5 0.0 reduce-scatter.2.cloned.1.call-start
  128.5 0.0 copy-done.4
  128.5 0.6 reduce_sum.36
  129.2 0.7 add_compare_fusion
  129.8 0.0 copy-done.3
  129.8 0.1 fusion.20
  129.9 7.9 %all-to-all-done = bf16[8,16,1024]{2,1,0:T(8,128)(2,1)S(1)} async-done(((bf16[8,16,1024]{2,1,0:T(8,128)(2,1)}), bf16[8,16,1024]{2,1,0:T(8,128)(2,1)S(1)}, u32[]{:S(2)}, u32[]{:S(2)}) %all-to-all-start) | async-done | bytes 262176 | tf_op jit(solution)/shard_map/all_to_all | solution.py:21
  137.8 0.0 copy-start.1
  137.9 0.0 copy-done
  137.9 0.0 slice-start
  137.9 1.0 multiply_reduce_fusion
  138.9 0.0 copy-done.2
  138.9 0.6 copy-done.1
  139.4 0.0 slice-start.1
  139.4 1.5 fusion.7
  140.9 0.0 slice-start.2
  141.0 1.1 fusion
  142.1 11.8 %all_to_all.38 = bf16[16,8,1024]{2,0,1:T(8,128)(2,1)S(1)} all-to-all(bf16[16,8,1024]{2,0,1:T(8,128)(2,1)S(1)} %bitcast.20), channel_id=1, replica_groups=mesh['grp'=2,'dp'=4,'sp'=4] {'grp','sp'}, dimensions={1} | all-to-all | bytes 524288 | tf_op jit(solution)/shard_map/all_to_all | solution.py:42
  153.9 0.0 slice-done
  153.9 0.0 slice-done.1
  153.9 0.0 slice-done.2
  153.9 4.6 %convolution_convert_fusion = bf16[128,5120]{1,0:T(8,128)(2,1)} fusion(bf16[128,1024]{1,0:T(8,128)(2,1)S(1)} %bitcast.18, bf16[5120,1024]{1,0:T(8,128)(2,1)S(1)} %bitcast.16), kind=kOutput, calls=%fused_computation.3 | convolution fusion | flops 1342832640 | bytes 12058624 | tf_op jit(solution)/shard_map/dot_general | solution.py:43
  158.5 0.0 reduce-scatter.2.cloned.1.call-update
  158.6 39.6 %psum.7 = f32[8192]{0:T(1024)} all-reduce(f32[8192]{0:T(1024)S(1)} %get-tuple-element.2), channel_id=1, replica_groups=mesh['grp'=2,'dp'=4,'sp'=4] {'grp','dp','sp'}, use_global_device_ids=true, to_apply=%region_6.7 | all-reduce | flops 8192 | bytes 65536 | tf_op jit(solution)/shard_map/psum | solution.py:49
  198.1 0.0 reduce-scatter.2.cloned.1.call-done
  (5 shorter events, 0.1 us)
Async XLA Ops:
  7.2 110.3 %all-gather.2.cloned.1.call-start = ((), (), s32[]{:S(2)}) async-start(), calls=%async_computation.3 | async-start | bytes 13107200 | tf_op jit(solution)/shard_map/all_gather | solution.py:19
  7.9 7.5 %collective-permute-start = (bf16[16,5120]{1,0:T(8,128)(2,1)}, bf16[16,5120]{1,0:T(8,128)(2,1)S(1)}, u32[]{:S(2)}, u32[]{:S(2)}) collective-permute-start(bf16[16,5120]{1,0:T(8,128)(2,1)} %param.7), channel_id=1, source_target_pairs={{0,1},{1,0},{2,3},{3,2},{16,17},{17,16},{18,19},{19,18},{4,5},{5,4... | collective-permute-start | bytes 491528 | tf_op jit(solution)/shard_map/ppermute | solution.py:13
  16.5 16.9 %collective-permute-start.1 = (bf16[32,5120]{1,0:T(8,128)(2,1)S(1)}, bf16[32,5120]{1,0:T(8,128)(2,1)S(1)}, u32[]{:S(2)}, u32[]{:S(2)}) collective-permute-start(bf16[32,5120]{1,0:T(8,128)(2,1)S(1)} %maximum_select_fusion.5), channel_id=1, source_target_pairs={{0,2},{1,3},{2,0},{3,1},{16,18},{17,19},{18,16},{19,17},{4,6},{5,7... | collective-permute-start | bytes 983048 | tf_op jit(solution)/shard_map/ppermute | solution.py:13
  33.5 2.2 %collective-permute-start.2 = (bf16[64,5120]{1,0:T(8,128)(2,1)S(1)}, bf16[64,5120]{1,0:T(8,128)(2,1)S(1)}, u32[]{:S(2)}, u32[]{:S(2)}) collective-permute-start(bf16[64,5120]{1,0:T(8,128)(2,1)S(1)} %maximum_select_fusion.4), channel_id=1, source_target_pairs={{0,16},{1,17},{2,18},{3,19},{16,0},{17,1},{18,2},{19,3},{4,20},{5,... | collective-permute-start | bytes 1966088 | tf_op jit(solution)/shard_map/ppermute | solution.py:13
  33.5 95.0 %copy-start.4 = (s32[8]{0:T(128)S(1)}, s32[8]{0:T(128)}, u32[]{:S(2)}) copy-start(s32[8]{0:T(128)} %param.9) | copy-start | bytes 100
  33.6 96.3 %copy-start.3 = (s32[16]{0:T(128)S(1)}, s32[16]{0:T(128)}, u32[]{:S(2)}) copy-start(s32[16]{0:T(128)} %param.10) | copy-start | bytes 196
  33.6 104.3 %copy-start = (bf16[128,8192]{1,0:T(8,128)(2,1)S(1)}, bf16[128,8192]{1,0:T(8,128)(2,1)}, u32[]{:S(2)}) copy-start(bf16[128,8192]{1,0:T(8,128)(2,1)} %param.11) | copy-start | bytes 6291460
  123.7 15.1 %copy-start.2 = (f32[8192]{0:T(1024)S(1)}, f32[8192]{0:T(1024)}, u32[]{:S(2)}) copy-start(f32[8192]{0:T(1024)} %param.13) | copy-start | bytes 98308
  123.7 14.1 %all-to-all-start = ((bf16[8,16,1024]{2,1,0:T(8,128)(2,1)}), bf16[8,16,1024]{2,1,0:T(8,128)(2,1)S(1)}, u32[]{:S(2)}, u32[]{:S(2)}) async-start(bf16[8,16,1024]{2,1,0:T(8,128)(2,1)} %bitcast), calls=%async_computation | async-start | bytes 524288 | tf_op jit(solution)/shard_map/all_to_all | solution.py:21
  128.5 69.7 %reduce-scatter.2.cloned.1.call-start = ((), (), s32[]{:S(2)}) async-start(), calls=%async_computation.4 | async-start | bytes 1474560 | tf_op jit(solution)/shard_map/reduce_scatter | solution.py:46
  137.8 1.6 copy-start.1
  137.9 16.0 %slice-start = ((s8[10485760]{0:T(1024)(128)(4,1)}), s8[4194304]{0:T(1024)(128)(4,1)S(1)}, s32[]{:S(2)}) async-start(s8[10485760]{0:T(1024)(128)(4,1)} %bitcast.15), calls=%async_computation.5 | async-start | bytes 8388608
  139.4 14.5 %slice-start.1 = ((s8[10485760]{0:T(1024)(128)(4,1)}), s8[4194304]{0:T(1024)(128)(4,1)S(1)}, s32[]{:S(2)}) async-start(s8[10485760]{0:T(1024)(128)(4,1)} %bitcast.15), calls=%async_computation.6 | async-start | bytes 8388608
  140.9 13.0 %slice-start.2 = ((s8[10485760]{0:T(1024)(128)(4,1)}), s8[2097152]{0:T(1024)(128)(4,1)S(1)}, s32[]{:S(2)}) async-start(s8[10485760]{0:T(1024)(128)(4,1)} %bitcast.15), calls=%async_computation.7 | async-start | bytes 4194304
Sparse Core Ops, SparseCore 0:
  9.8 107.6 all-gather.1
  158.7 35.0 reduce-scatter.1
